TPU v7x, 32 devices: a whole 2x2x4 slice. The times are simulated.
32 devices in a mesh: fsdp: 4 (over y, x), seq: 8 (over z, core).
Axes of the slice: x: 2, y: 2, z: 4, core: 2. Of those that a mesh axis runs over, the one named last changes fastest.
Arguments:
- block_input: float32 [4, 1024, 1024], P('fsdp', 'seq'), may hold values from -6 to 6
- norm_gain: float32 [1024], replicated, may hold values from 0.5 to 1.5
- w_in: bfloat16 [1024, 4384], P('fsdp', 'seq'), may hold values from -0.1875 to 0.1875
- conv_w: float32 [4, 2304], replicated, may hold values from -0.5 to 0.5
- conv_b: float32 [2304], replicated, may hold values from -0.5 to 0.5
- dt_bias: float32 [32], replicated, may hold values from -6.5 to -2.5
- a_log: float32 [32], replicated, may hold values from 0 to 2.77
- skip_gain: float32 [32], replicated, may hold values from 0.5 to 1.5
- gate_gain: float32 [2048], replicated, may hold values from 0.5 to 1.5
- w_out: bfloat16 [2048, 1024], P('fsdp', 'seq'), may hold values from -0.125 to 0.125
- out_cotangent: float32 [4, 1024, 1024], P('fsdp', 'seq'), may hold values from -6 to 6
Outputs:
- block_output: float32 [4, 1024, 1024], P('fsdp', 'seq')
- grad_input: float32 [4, 1024, 1024], P('fsdp', 'seq')
- grad_norm_gain: float32 [1024], replicated
- grad_w_in: float32 [1024, 4384], P('fsdp', 'seq')
- grad_conv_w: float32 [4, 2304], replicated
- grad_conv_b: float32 [2304], replicated
- grad_dt_bias: float32 [32], replicated
- grad_a_log: float32 [32], replicated
- grad_skip_gain: float32 [32], replicated
- grad_gate_gain: float32 [2048], replicated
- grad_w_out: float32 [2048, 1024], P('fsdp', 'seq')
All inputs are finite; a program needn't handle non-finite values.
Results may differ from a plain program's by a relative error of at most 0.011.
Values may be sent and summed in bfloat16 or wider, within the bound.
No kernel may reach another device: no remote copies, remote signals or barrier semaphores. Data moves between devices by JAX's collectives and lax.ppermute only.
A program may use at most 128 MiB of HBM per device.

v0:
```python
import jax
import jax.numpy as jnp
from jax import lax
from jax.sharding import PartitionSpec as P

DI = 2048
HEADS = 32
HEAD_DIM = 64
STATE = 128
CONV_W = 4
GROUP = 128
EPS = 1e-05


def rms_apply(values, norm_gain):
    return values * lax.rsqrt(jnp.mean(values * values, axis=-1, keepdims=True) + EPS) * norm_gain


def gated_apply(values, gate_values, norm_gain):
    return rms_apply(values * jax.nn.silu(gate_values), norm_gain)


def causal_conv(signal, kernel, offset):
    taps = kernel.shape[0]
    length = signal.shape[0]
    padded = jnp.pad(signal, ((taps - 1, 0), (0, 0)))
    summed = offset + kernel[0] * padded[0:length]
    for tap_index in range(1, taps):
        summed = summed + kernel[tap_index] * padded[tap_index : tap_index + length]
    return jax.nn.silu(summed)


def state_space(signal, step_size, b_rows, c_rows, log_rate, skip_value):
    length = signal.shape[0]
    channels = signal.shape[1]
    blocks = length // GROUP
    highest = lax.Precision.HIGHEST
    decay_rate = -jnp.exp(log_rate) * step_size
    x_blocks = signal.reshape(blocks, GROUP, channels)
    step_blocks = step_size.reshape(blocks, GROUP)
    b_blocks = b_rows.reshape(blocks, GROUP, b_rows.shape[1])
    c_blocks = c_rows.reshape(blocks, GROUP, c_rows.shape[1])
    running = jnp.cumsum(decay_rate.reshape(blocks, GROUP), axis=1)
    scores = jnp.einsum("cin,cjn->cij", c_blocks, b_blocks, precision=highest)
    row_index = lax.broadcasted_iota(jnp.int32, (GROUP, GROUP), 0)
    col_index = lax.broadcasted_iota(jnp.int32, (GROUP, GROUP), 1)
    causal = row_index >= col_index
    spread = running[:, :, None] - running[:, None, :]
    decay = jnp.where(causal, jnp.exp(jnp.where(causal, spread, 0.0)), 0.0)
    within = jnp.einsum(
        "cij,cjp->cip", scores * decay * step_blocks[:, None, :], x_blocks, precision=highest
    )
    toward = jnp.exp(running[:, -1:] - running) * step_blocks
    inflow = jnp.einsum("cjp,cjn->cpn", x_blocks * toward[:, :, None], b_blocks, precision=highest)
    carried = jnp.exp(running[:, -1])

    def advance(memory, packet):
        factor, update = packet
        return (factor * memory + update, memory)

    _, openings = lax.scan(
        advance, jnp.zeros((channels, b_rows.shape[1]), signal.dtype), (carried, inflow)
    )
    across = jnp.exp(running)[:, :, None] * jnp.einsum(
        "cin,cpn->cip", c_blocks, openings, precision=highest
    )
    return (within + across).reshape(length, channels) + skip_value * signal


def mixer_head(
    x_raw,
    dt_raw,
    b_raw,
    c_raw,
    kern_x,
    bias_x,
    kern_b,
    bias_b,
    kern_c,
    bias_c,
    log_rate,
    skip_value,
    dt_shift,
):
    x_act = causal_conv(x_raw, kern_x, bias_x)
    b_act = causal_conv(b_raw, kern_b, bias_b)
    c_act = causal_conv(c_raw, kern_c, bias_c)
    step_size = jax.nn.softplus(dt_raw + dt_shift)
    return state_space(x_act, step_size, b_act, c_act, log_rate, skip_value)


def inner_rows(left, right):
    return lax.dot_general(
        left, right, (((0,), (0,)), ((), ())), preferred_element_type=jnp.float32
    )


def outer_cols(left, right):
    return lax.dot_general(
        left, right, (((1,), (1,)), ((), ())), preferred_element_type=jnp.float32
    )


def per_device(
    block_input,
    norm_gain,
    w_in,
    conv_w,
    conv_b,
    dt_bias,
    a_log,
    skip_gain,
    gate_gain,
    w_out,
    out_cotangent,
):
    residual = block_input[0]
    grad_out = out_cotangent[0]
    tokens = residual.shape[0]
    in_columns, out_columns = (
        lax.all_gather(w_in, "seq", axis=1, tiled=True),
        lax.all_gather(w_out, "seq", axis=1, tiled=True),
    )
    w_in_full, w_out_full = (
        lax.all_gather(in_columns, "fsdp", axis=0, tiled=True),
        lax.all_gather(out_columns, "fsdp", axis=0, tiled=True),
    )
    normed, norm_pull = jax.vjp(rms_apply, residual, norm_gain)
    normed_half = normed.astype(jnp.bfloat16)
    projected = jnp.dot(normed_half, w_in_full, preferred_element_type=jnp.float32).astype(
        jnp.bfloat16
    )
    gate_half = projected[:, :DI]
    inner_part = projected[:, DI : 2 * DI].reshape(tokens, HEADS, HEAD_DIM)
    step_part = projected[:, 2 * DI + 2 * STATE :]
    inner_heads, step_heads = (
        lax.all_to_all(inner_part, "seq", split_axis=1, concat_axis=0, tiled=True),
        lax.all_to_all(step_part, "seq", split_axis=1, concat_axis=0, tiled=True),
    )
    input_rows, output_rows = (
        lax.all_gather(projected[:, 2 * DI : 2 * DI + STATE], "seq", axis=0, tiled=True),
        lax.all_gather(
            projected[:, 2 * DI + STATE : 2 * DI + 2 * STATE], "seq", axis=0, tiled=True
        ),
    )
    local_heads = inner_heads.shape[1]
    head_start = lax.axis_index("seq") * local_heads
    kern_x = lax.dynamic_slice_in_dim(
        conv_w[:, :DI].reshape(CONV_W, HEADS, HEAD_DIM), head_start, local_heads, 1
    )
    bias_x = lax.dynamic_slice_in_dim(
        conv_b[:DI].reshape(HEADS, HEAD_DIM), head_start, local_heads, 0
    )
    kern_b = conv_w[:, DI : DI + STATE]
    kern_c = conv_w[:, DI + STATE :]
    bias_b = conv_b[DI : DI + STATE]
    bias_c = conv_b[DI + STATE :]
    rate_local = lax.dynamic_slice_in_dim(a_log, head_start, local_heads, 0)
    skip_local = lax.dynamic_slice_in_dim(skip_gain, head_start, local_heads, 0)
    shift_local = lax.dynamic_slice_in_dim(dt_bias, head_start, local_heads, 0)
    mixer_many = jax.vmap(
        mixer_head, in_axes=(1, 1, None, None, 1, 0, None, None, None, None, 0, 0, 0), out_axes=1
    )
    y_heads, mixer_pull = jax.vjp(
        mixer_many,
        inner_heads.astype(jnp.float32),
        step_heads.astype(jnp.float32),
        input_rows.astype(jnp.float32),
        output_rows.astype(jnp.float32),
        kern_x,
        bias_x,
        kern_b,
        bias_b,
        kern_c,
        bias_c,
        rate_local,
        skip_local,
        shift_local,
    )
    y_tokens = lax.all_to_all(
        y_heads.astype(jnp.bfloat16), "seq", split_axis=0, concat_axis=1, tiled=True
    ).reshape(tokens, DI)
    gated, gate_pull = jax.vjp(
        gated_apply, y_tokens.astype(jnp.float32), gate_half.astype(jnp.float32), gate_gain
    )
    gated_half = gated.astype(jnp.bfloat16)
    block_out = residual + jnp.dot(gated_half, w_out_full, preferred_element_type=jnp.float32)
    cot_half = grad_out.astype(jnp.bfloat16)
    w_in_back, w_out_back = (w_in_full, w_out_full)
    g_w_out = inner_rows(gated_half, cot_half)
    dgated = outer_cols(cot_half, w_out_back)
    grad_y, grad_z, g_gate = gate_pull(dgated)
    dy_heads = lax.all_to_all(
        grad_y.astype(jnp.bfloat16).reshape(tokens, HEADS, HEAD_DIM),
        "seq",
        split_axis=1,
        concat_axis=0,
        tiled=True,
    )
    pieces = mixer_pull(dy_heads.astype(jnp.float32))
    g_xr, g_dtr, g_br, g_cr, g_kx, g_bx, g_kb, g_bb, g_kc, g_bc, g_rate, g_skip, g_shift = pieces
    dx_tokens, ddt_tokens = (
        lax.all_to_all(g_xr.astype(jnp.bfloat16), "seq", split_axis=0, concat_axis=1, tiled=True),
        lax.all_to_all(g_dtr.astype(jnp.bfloat16), "seq", split_axis=0, concat_axis=1, tiled=True),
    )
    db_tokens, dc_tokens = (
        lax.psum_scatter(g_br, "seq", scatter_dimension=0, tiled=True),
        lax.psum_scatter(g_cr, "seq", scatter_dimension=0, tiled=True),
    )
    dproj = jnp.concatenate(
        [
            grad_z.astype(jnp.bfloat16),
            dx_tokens.reshape(tokens, DI),
            db_tokens.astype(jnp.bfloat16),
            dc_tokens.astype(jnp.bfloat16),
            ddt_tokens,
        ],
        axis=1,
    )
    g_w_in = inner_rows(normed_half, dproj)
    dnormed = outer_cols(dproj, w_in_back)
    du_norm, g_norm = norm_pull(dnormed)
    grad_in = grad_out + du_norm
    rows_in, rows_out = (
        lax.psum_scatter(g_w_in, "fsdp", scatter_dimension=0, tiled=True),
        lax.psum_scatter(g_w_out, "fsdp", scatter_dimension=0, tiled=True),
    )
    owned_w_in, owned_w_out = (
        lax.psum_scatter(rows_in, "seq", scatter_dimension=1, tiled=True),
        lax.psum_scatter(rows_out, "seq", scatter_dimension=1, tiled=True),
    )
    kern_full = lax.dynamic_update_slice_in_dim(
        jnp.zeros((CONV_W, HEADS, HEAD_DIM), jnp.float32), g_kx, head_start, 1
    ).reshape(CONV_W, DI)
    g_conv_w = jnp.concatenate([kern_full, g_kb, g_kc], axis=1)
    offset_full = lax.dynamic_update_slice_in_dim(
        jnp.zeros((HEADS, HEAD_DIM), jnp.float32), g_bx, head_start, 0
    ).reshape(DI)
    g_conv_b = jnp.concatenate([offset_full, g_bb, g_bc])
    shift_full = lax.dynamic_update_slice_in_dim(
        jnp.zeros((HEADS,), jnp.float32), g_shift, head_start, 0
    )
    rate_full = lax.dynamic_update_slice_in_dim(
        jnp.zeros((HEADS,), jnp.float32), g_rate, head_start, 0
    )
    skip_full = lax.dynamic_update_slice_in_dim(
        jnp.zeros((HEADS,), jnp.float32), g_skip, head_start, 0
    )
    summed = lax.psum(
        (g_norm, g_conv_w, g_conv_b, shift_full, rate_full, skip_full, g_gate), ("fsdp", "seq")
    )
    return (
        block_out[None],
        grad_in[None],
        summed[0],
        owned_w_in,
        summed[1],
        summed[2],
        summed[3],
        summed[4],
        summed[5],
        summed[6],
        owned_w_out,
    )


def solution(mesh):
    return jax.shard_map(
        per_device,
        mesh=mesh,
        in_specs=(
            P("fsdp", "seq", None),
            P(),
            P("fsdp", "seq"),
            P(),
            P(),
            P(),
            P(),
            P(),
            P(),
            P("fsdp", "seq"),
            P("fsdp", "seq", None),
        ),
        out_specs=(
            P("fsdp", "seq", None),
            P("fsdp", "seq", None),
            P(),
            P("fsdp", "seq"),
            P(),
            P(),
            P(),
            P(),
            P(),
            P(),
            P("fsdp", "seq"),
        ),
        check_vma=False,
    )
```

profile of v0, /device:TPU:0, one launch (start us, length us, event | category | flops | bytes accessed | tf_op | source)
XLA Modules:
  0.0 822.4 jit_solution(4524585330081583033)
XLA Ops:
  8.7 34.2 %all-gather.12.cloned.1.call-done = bf16[8,548,256]{2,1,0:T(8,128)(2,1)} async-done(((bf16[1,548,256]{2,1,0:T(8,128)(2,1)}), bf16[8,548,256]{2,1,0:T(8,128)(2,1)}) %all-gather.12.cloned.1.call-update) | async-done | bytes 2244624 | tf_op jit(solution)/shard_map/all_gather | solution.py:121
  50.7 17.1 %all-gather.8.cloned.1.call-done = bf16[512,1024]{1,0:T(8,128)(2,1)} async-done(((bf16[512,128]{1,0:T(8,128)(2,1)}), bf16[512,1024]{1,0:T(8,128)(2,1)}) %all-gather.8.cloned.1.call-update) | async-done | bytes 1048592 | tf_op jit(solution)/shard_map/all_gather | solution.py:122
  67.8 92.8 %all-gather.6.cloned.1.call-done = bf16[1024,4384]{0,1:T(8,128)(2,1)} async-done(((bf16[256,4384]{0,1:T(8,128)(2,1)}), bf16[1024,4384]{0,1:T(8,128)(2,1)}) %all-gather.6.cloned.1.call-update) | async-done | bytes 8978448 | tf_op jit(solution)/shard_map/all_gather | solution.py:125
  160.7 6.1 convolution_convert_fusion
  167.5 4.6 all-to-all-start
  172.1 13.6 %all_gather.21 = bf16[1024,128]{0,1:T(8,128)(2,1)S(1)} all-gather(bf16[128,128]{0,1:T(8,128)(2,1)S(1)} %get-tuple-element.340), channel_id=1, replica_groups=mesh['fsdp'=4,'seq'=8] {'seq'}, dimensions={0}, use_global_device_ids=true | all-gather | bytes 294912 | tf_op jit(solution)/shard_map/all_gather | solution.py:141
  185.8 13.1 %all_gather.20 = bf16[1024,128]{0,1:T(8,128)(2,1)S(1)} all-gather(bf16[128,128]{0,1:T(8,128)(2,1)S(1)} %get-tuple-element.339), channel_id=1, replica_groups=mesh['fsdp'=4,'seq'=8] {'seq'}, dimensions={0}, use_global_device_ids=true | all-gather | bytes 294912 | tf_op jit(solution)/shard_map/all_gather | solution.py:142
  205.9 4.7 all-to-all-start.1
  218.3 7.6 all-to-all-done.1
  232.3 23.3 %while.34 = (s32[]{:T(128)}, f32[4,64,128]{2,1,0:T(8,128)S(1)}, f32[8,4,64,128]{3,2,1,0:T(8,128)S(1)}, f32[8,4,1,1]{1,3,2,0:T(1,128)}, f32[8,4]{1,0:T(8,128)}, /...) while((s32[]{:T(128)}, f32[4,64,128]{2,1,0:T(8,128)S(1)}, f32[8,4,64,128]{3,2,1,0:T(8,128)S(1)}, ...), condition=%wide.region_3.4_spmd.clone, body=%wide.region_2.3_spmd.clone.sunk | while | flops 131075 | bytes 656552 | solution.py:61
  265.8 19.6 %all_to_all.83 = bf16[8,2,16384]{2,1,0:T(2,128)(2,1)} all-to-all(bf16[8,2,16384]{2,1,0:T(2,128)(2,1)} %reshape.324), channel_id=1, replica_groups=mesh['fsdp'=4,'seq'=8] {'seq'}, dimensions={0} | all-to-all | bytes 1048576 | tf_op jit(solution)/shard_map/all_to_all | solution.py:180
  304.9 15.3 %all-to-all-done.3 = bf16[128,32,64]{0,2,1:T(8,128)(2,1)} async-done(((bf16[128,32,64]{0,2,1:T(8,128)(2,1)}), bf16[128,32,64]{0,2,1:T(8,128)(2,1)}, u32[]{:S(2)}, u32[]{:S(2)}) %all-to-all-start.3) | async-done | bytes 524320 | tf_op jit(solution)/shard_map/all_to_all | solution.py:193
  321.5 5.2 fusion.18
  334.5 34.1 %while.35 = (s32[]{:T(128)}, f32[4,64,128]{2,1,0:T(8,128)S(1)}, f32[8,4]{1,0:T(8,128)}, f32[8,4,64,128]{3,2,1,0:T(8,128)}, f32[8,4,64,128]{3,2,1,0:T(8,128)}, /*...) while((s32[]{:T(128)}, f32[4,64,128]{2,1,0:T(8,128)S(1)}, ...), condition=%wide.region_8.9_spmd.clone, body=%wide.region_6.8_spmd.clone.sunk | while | flops 196608 | bytes 786676 | solution.py:61
  379.7 5.1 multiply_reduce_fusion.10
  409.4 5.0 reduce_window_sum.23
  415.2 8.1 all-to-all-done.4
  431.1 16.9 %reduce-scatter.10.cloned.1.call-done = f32[128,128]{0,1:T(8,128)} async-done(((f32[1024,128]{0,1:T(8,128)}), f32[128,128]{0,1:T(8,128)}) %reduce-scatter.10.cloned.1.call-update) | async-done | bytes 65552 | tf_op jit(solution)/shard_map/reduce_scatter | solution.py:208
  448.9 9.2 %fusion.92 = f32[1024,4384]{0,1:T(8,128)} fusion(bf16[128,4384]{0,1:T(8,128)(2,1)S(1)} %constant_dynamic-update-slice_fusion.1, f32[1,128,1024]{2,1,0:T(8,128)S(1)} %copy-done, f32[1024]{0:T(1024)S(1)} %copy-done.36, f32[128]{0:T(128)S(1)} %copy-done.60), kind=kOutput, calls=%fused_computation.241 | convolution fusion | flops 1149632512 | bytes 19608064 | tf_op jit(solution)/shard_map/dot_general | solution.py:93
  465.3 5.3 multiply_reduce_fusion.16
  470.7 64.6 %reduce-scatter.14.cloned.1.call-done = f32[512,1024]{1,0:T(8,128)} async-done(((f32[2048,1024]{1,0:T(8,128)}), f32[512,1024]{1,0:T(8,128)}) %reduce-scatter.14.cloned.1.call-update) | async-done | bytes 2097168 | tf_op jit(solution)/shard_map/reduce_scatter | solution.py:226
  535.3 166.4 %reduce-scatter.12.cloned.1.call-done = f32[256,4384]{0,1:T(8,128)} async-done(((f32[1024,4384]{0,1:T(8,128)}), f32[256,4384]{0,1:T(8,128)}) %reduce-scatter.12.cloned.1.call-update) | async-done | bytes 4489232 | tf_op jit(solution)/shard_map/reduce_scatter | solution.py:225
  701.7 70.2 %fusion = f32[256,552]{0,1:T(8,128)S(1)} fusion(f32[256,4384]{0,1:T(8,128)} %reduce-scatter.12.cloned.1.call-done), kind=kCustom, calls=%all-reduce-scatter | all-reduce-scatter fusion | flops 1130497 | bytes 5054976
  774.3 39.7 %all-reduce.31 = (f32[1024]{0:T(1024)}, f32[4,2304]{1,0:T(4,128)}, f32[2304]{0:T(1024)}, f32[32]{0:T(128)}, f32[32]{0:T(128)}, /*index=5*/f32[32]{0:T(128)}, f32[2048]{0:T(1024)}) all-reduce(f32[1024]{0:T(1024)S(1)} %get-tuple-element.282, f32[4,2304]{1,0:T(4,128)S(1)} %pad_maximum_fusion, ...), channel_id=1, replica_groups=mesh['fsdp'=4,'seq'=8] {'fsdp','seq'}, use_global_device_ids=true, to_apply=%region_21.22 | all-reduce | flops 14688 | bytes 117504 | tf_op jit(solution)/shard_map/psum | solution.py:249
  (417 shorter events, 181.3 us)
Async XLA Ops:
  7.2 35.7 %all-gather.12.cloned.1.call-start = ((), (), s32[]{:S(2)}) async-start(), calls=%async_computation.19 | async-start | bytes 2543616 | tf_op jit(solution)/shard_map/all_gather | solution.py:121
  7.9 59.9 %all-gather.8.cloned.1.call-start = ((), (), s32[]{:S(2)}) async-start(), calls=%async_computation.12 | async-start | bytes 1179648 | tf_op jit(solution)/shard_map/all_gather | solution.py:122
  8.7 152.0 %all-gather.6.cloned.1.call-start = ((), (), s32[]{:S(2)}) async-start(), calls=%async_computation.11 | async-start | bytes 11223040 | tf_op jit(solution)/shard_map/all_gather | solution.py:125
  47.0 246.5 %all-gather.10.cloned.1.call-start = ((), (), s32[]{:S(2)}) async-start(), calls=%async_computation.13 | async-start | bytes 5242880 | tf_op jit(solution)/shard_map/all_gather | solution.py:126
  47.9 167.0 %copy-start.79 = (f32[4]{0:T(128)}, f32[4]{0:T(128)S(1)}, u32[]{:S(2)}) copy-start(f32[4]{0:T(128)S(1)} %dynamic_slice.52) | copy-start | bytes 52
  48.6 166.3 %copy-start.81 = (f32[4]{0:T(128)}, f32[4]{0:T(128)S(1)}, u32[]{:S(2)}) copy-start(f32[4]{0:T(128)S(1)} %fusion.87) | copy-start | bytes 52
  50.6 148.4 %copy-start.71 = (f32[128]{0:T(128)}, f32[128]{0:T(128)S(1)}, u32[]{:S(2)}) copy-start(f32[128]{0:T(128)S(1)} %get-tuple-element.363) | copy-start | bytes 1540
  50.6 148.4 %copy-start.73 = (f32[128]{0:T(128)}, f32[128]{0:T(128)S(1)}, u32[]{:S(2)}) copy-start(f32[128]{0:T(128)S(1)} %get-tuple-element.364) | copy-start | bytes 1540
  50.6 149.8 %copy-start.63 = (f32[128]{0:T(128)}, f32[128]{0:T(128)S(1)}, u32[]{:S(2)}) copy-start(f32[128]{0:T(128)S(1)} %get-tuple-element.362) | copy-start | bytes 1540
  50.6 149.8 %copy-start.65 = (f32[128]{0:T(128)}, f32[128]{0:T(128)S(1)}, u32[]{:S(2)}) copy-start(f32[128]{0:T(128)S(1)} %get-tuple-element.366) | copy-start | bytes 1540
  50.6 149.8 %copy-start.67 = (f32[128]{0:T(128)}, f32[128]{0:T(128)S(1)}, u32[]{:S(2)}) copy-start(f32[128]{0:T(128)S(1)} %get-tuple-element.367) | copy-start | bytes 1540
  50.6 149.8 %copy-start.69 = (f32[128]{0:T(128)}, f32[128]{0:T(128)S(1)}, u32[]{:S(2)}) copy-start(f32[128]{0:T(128)S(1)} %get-tuple-element.368) | copy-start | bytes 1540
  167.5 38.4 %all-to-all-start = ((bf16[128,8,4]{0,2,1:T(4,128)(2,1)}), bf16[128,8,4]{0,2,1:T(4,128)(2,1)S(1)}, u32[]{:S(2)}, u32[]{:S(2)}) async-start(bf16[128,8,4]{0,2,1:T(4,128)(2,1)} %bitcast.12), calls=%async_computation | async-start | bytes 16384 | tf_op jit(solution)/shard_map/all_to_all | solution.py:138
  205.9 20.0 %all-to-all-start.1 = ((bf16[128,32,64]{0,2,1:T(8,128)(2,1)}), bf16[128,32,64]{0,2,1:T(8,128)(2,1)}, u32[]{:S(2)}, u32[]{:S(2)}) async-start(bf16[128,32,64]{0,2,1:T(8,128)(2,1)} %bitcast.444), calls=%async_computation.1 | async-start | bytes 1048576 | tf_op jit(solution)/shard_map/all_to_all | solution.py:137
  300.7 19.5 %all-to-all-start.3 = ((bf16[128,32,64]{0,2,1:T(8,128)(2,1)}), bf16[128,32,64]{0,2,1:T(8,128)(2,1)}, u32[]{:S(2)}, u32[]{:S(2)}) async-start(bf16[128,32,64]{0,2,1:T(8,128)(2,1)} %bitcast.447), calls=%async_computation.3 | async-start | bytes 1048576 | tf_op jit(solution)/shard_map/all_to_all | solution.py:193
  304.9 125.4 %reduce-scatter.8.cloned.1.call-start = ((), (), s32[]{:S(2)}) async-start(), calls=%async_computation.14 | async-start | bytes 589824 | tf_op jit(solution)/shard_map/reduce_scatter | solution.py:207
  386.4 61.7 %reduce-scatter.10.cloned.1.call-start = ((), (), s32[]{:S(2)}) async-start(), calls=%async_computation.15 | async-start | bytes 589824 | tf_op jit(solution)/shard_map/reduce_scatter | solution.py:208
  388.0 147.3 %reduce-scatter.14.cloned.1.call-start = ((), (), s32[]{:S(2)}) async-start(), calls=%async_computation.17 | async-start | bytes 10485760 | tf_op jit(solution)/shard_map/reduce_scatter | solution.py:226
  404.2 19.1 %all-to-all-start.4 = ((bf16[8,2,16384]{2,1,0:T(2,128)(2,1)}), bf16[8,2,16384]{2,1,0:T(2,128)(2,1)S(1)}, u32[]{:S(2)}, u32[]{:S(2)}) async-start(bf16[8,2,16384]{2,1,0:T(2,128)(2,1)} %reshape.326), calls=%async_computation.4 | async-start | bytes 1048576 | tf_op jit(solution)/shard_map/all_to_all | solution.py:203
  423.3 25.6 %all-to-all-start.5 = ((bf16[8,128,4]{1,2,0:T(4,128)(2,1)}), bf16[8,128,4]{1,2,0:T(4,128)(2,1)S(1)}, u32[]{:S(2)}, u32[]{:S(2)}) async-start(bf16[8,128,4]{1,2,0:T(4,128)(2,1)} %bitcast.385), calls=%async_computation.7 | async-start | bytes 16384 | tf_op jit(solution)/shard_map/all_to_all | solution.py:204
  426.6 275.1 %reduce-scatter.12.cloned.1.call-start = ((), (), s32[]{:S(2)}) async-start(), calls=%async_computation.16 | async-start | bytes 22446080 | tf_op jit(solution)/shard_map/reduce_scatter | solution.py:225
  458.1 357.3 %reduce-scatter.16.cloned.1.call-start = ((), (), s32[]{:S(2)}) async-start(), calls=%async_computation.18 | async-start | bytes 2359296 | tf_op jit(solution)/shard_map/reduce_scatter | solution.py:230
  535.3 238.0 %copy-start.15 = (f32[1,128,1024]{2,1,0:T(8,128)S(1)}, f32[1,128,1024]{2,1,0:T(8,128)}, u32[]{:S(2)}) copy-start(f32[1,128,1024]{2,1,0:T(8,128)} %param.25) | copy-start | bytes 1572868
  772.0 42.0 %collective-permute-start = (f32[256,28]{0,1:T(8,128)S(1)}, f32[256,28]{0,1:T(8,128)S(1)}, u32[]{:S(2)}, u32[]{:S(2)}) collective-permute-start(f32[256,28]{0,1:T(8,128)S(1)} %slice.156), channel_id=1, source_target_pairs={{0,1},{1,2},{2,3},{3,4},{4,5},{5,6},{6,7},{8,9},{9,10},{10,11},{11... | collective-permute-start | bytes 86024
  (95 other events, 1122.3 us)
Sparse Core Ops, SparseCore 0:
  9.6 33.2 all-gather.11
  44.5 23.2 all-gather.7
  69.6 90.9 all-gather.5
  162.3 52.5 all-gather.9
  386.5 29.5 reduce-scatter.7
  418.2 29.7 reduce-scatter.9
  451.1 84.1 reduce-scatter.13
  538.4 163.2 reduce-scatter.11
  704.6 50.0 reduce-scatter.15
where the time goes:
time: 830 us; the launch traced here: 822 us
  waiting for transfers between devices  425 us (51%)
  blocking collectives  156 us (19%)
  local copies, waits for them, and re-layouts  71.1 us (9%)
  matrix products  66 us (8%)
  other arithmetic  65.5 us (8%)
  starting transfers between devices  22.4 us (3%)
  between operations  16.5 us (2%)
    reduce_scatter x1, waiting for transfers between devices, per_device(): lax.psum_scatter(g_w_in, 'fsdp', scatter_dimension=0, tiled=True)  166 us
    all_gather x1, waiting for transfers between devices, per_device(): lax.all_gather(in_columns, 'fsdp', axis=0, tiled=True)  92.8 us
    unnamed x1, blocking collectives  70.2 us
    reduce_scatter x1, waiting for transfers between devices, per_device(): lax.psum_scatter(g_w_out, 'fsdp', scatter_dimension=0, tiled=True)  64.6 us
    psum x1, blocking collectives, per_device(): lax.psum((g_norm, g_conv_w, g_conv_b, shift_full, rate_full, skip_full, g...  39.7 us
    all_gather x1, waiting for transfers between devices, per_device(): lax.all_gather(w_in, 'seq', axis=1, tiled=True)  34.2 us
    unnamed x221, local copies, waits for them, and re-layouts  21.2 us
    dynamic_update_slice x16, local copies, waits for them, and re-layouts, state_space(): lax.scan(advance, jnp.zeros((channels, b_rows.shape[1]), signal.dtype), (...  19.9 us
  transfers between devices with their start and end apart: 15, of which 9 were waited for; matrix products, arithmetic and copies ran while one was open for 24% of the time, Pallas kernels for 0%

commit v1 on v0

--- a/solution.py
+++ b/solution.py
@@ -10,6 +10,18 @@
 CONV_W = 4
 GROUP = 128
 EPS = 1e-05
+
+
+def doubled_up(x, axis, dim):
+    ways, here, hop = (lax.axis_size(axis), lax.axis_index(axis), x.shape[dim])
+    line, have = (x, 1)
+    while have < ways:
+        line = jnp.concatenate(
+            [line, lax.ppermute(line, axis, [(d, (d - have) % ways) for d in range(ways)])],
+            axis=dim,
+        )
+        have = 2 * have
+    return jnp.roll(line, here * hop, axis=dim)
 
 
 def rms_apply(values, norm_gain):
@@ -122,7 +134,7 @@
         lax.all_gather(w_out, "seq", axis=1, tiled=True),
     )
     w_in_full, w_out_full = (
-        lax.all_gather(in_columns, "fsdp", axis=0, tiled=True),
+        doubled_up(in_columns, "fsdp", 0),
         lax.all_gather(out_columns, "fsdp", axis=0, tiled=True),
     )
     normed, norm_pull = jax.vjp(rms_apply, residual, norm_gain)

time: 830 us -> 898 us (1.082)
  waiting for transfers between devices: 425 us -> 496 us
    ppermute x0 -> x2, waiting for transfers between devices: none -> 154 us  [doubled_up(): lax.ppermute(line, axis, [(d, (d - have) % ways) for d in range(ways)])]
    all_gather x1 -> x0, waiting for transfers between devices: 92.8 us -> none  [per_device(): lax.all_gather(in_columns, 'fsdp', axis=0, tiled=True)]
    unnamed x221 -> x232, local copies, waits for them, and re-layouts: 21.2 us -> 26.2 us
  transfers between devices with their start and end apart: 15 -> 16, of which waited for: 9 -> 10; matrix products, arithmetic and copies ran while one was open for 24% -> 20% of each run, Pallas kernels for 0% -> 0%
where the time goes in v1:
time: 898 us; the launch traced here: 889 us
  waiting for transfers between devices  496 us (55%)
  blocking collectives  156 us (17%)
  other arithmetic  68 us (8%)
  local copies, waits for them, and re-layouts  63.9 us (7%)
  matrix products  61.7 us (7%)
  starting transfers between devices  25.6 us (3%)
  between operations  17 us (2%)
    reduce_scatter x1, waiting for transfers between devices, per_device(): lax.psum_scatter(g_w_in, 'fsdp', scatter_dimension=0, tiled=True)  166 us
    ppermute x2, waiting for transfers between devices, doubled_up(): lax.ppermute(line, axis, [(d, (d - have) % ways) for d in range(ways)])  154 us
    unnamed x1, blocking collectives  70.2 us
    reduce_scatter x1, waiting for transfers between devices, per_device(): lax.psum_scatter(g_w_out, 'fsdp', scatter_dimension=0, tiled=True)  64.8 us
    psum x1, blocking collectives, per_device(): lax.psum((g_norm, g_conv_w, g_conv_b, shift_full, rate_full, skip_full, g...  39.7 us
    all_gather x1, waiting for transfers between devices, per_device(): lax.all_gather(w_in, 'seq', axis=1, tiled=True)  34.9 us
    unnamed x232, local copies, waits for them, and re-layouts  26.2 us
    all_gather x1, waiting for transfers between devices, per_device(): lax.all_gather(w_out, 'seq', axis=1, tiled=True)  22.2 us
  transfers between devices with their start and end apart: 16, of which 10 were waited for; matrix products, arithmetic and copies ran while one was open for 20% of the time, Pallas kernels for 0%

profile of v1, /device:TPU:0, one launch (start us, length us, event | category | flops | bytes accessed | tf_op | source)
XLA Modules:
  0.0 888.9 jit_solution(8210799760071093894)
XLA Ops:
  8.0 34.9 %all-gather.9.cloned.1.call-done = bf16[8,548,256]{2,1,0:T(8,128)(2,1)} async-done(((bf16[1,548,256]{2,1,0:T(8,128)(2,1)}), bf16[8,548,256]{2,1,0:T(8,128)(2,1)}) %all-gather.9.cloned.1.call-update) | async-done | bytes 2244624 | tf_op jit(solution)/shard_map/all_gather | solution.py:133
  48.0 48.5 %collective-permute-done = bf16[256,4384]{0,1:T(8,128)(2,1)S(1)} collective-permute-done((bf16[256,4384]{0,1:T(8,128)(2,1)S(1)}, bf16[256,4384]{0,1:T(8,128)(2,1)S(1)}, u32[]{:S(2)}, u32[]{:S(2)}) %collective-permute-start) | collective-permute-done | bytes 2244640 | tf_op jit(solution)/shard_map/ppermute | solution.py:20
  102.2 22.2 %all-gather.5.cloned.1.call-done = bf16[512,1024]{1,0:T(8,128)(2,1)} async-done(((bf16[512,128]{1,0:T(8,128)(2,1)}), bf16[512,1024]{1,0:T(8,128)(2,1)}) %all-gather.5.cloned.1.call-update) | async-done | bytes 1048592 | tf_op jit(solution)/shard_map/all_gather | solution.py:134
  126.3 105.1 %collective-permute-done.1 = bf16[512,4384]{0,1:T(8,128)(2,1)} collective-permute-done((bf16[512,4384]{0,1:T(8,128)(2,1)}, bf16[512,4384]{0,1:T(8,128)(2,1)}, u32[]{:S(2)}, u32[]{:S(2)}) %collective-permute-start.1) | collective-permute-done | bytes 4489248 | tf_op jit(solution)/shard_map/ppermute | solution.py:20
  245.5 13.1 %all_gather.16 = bf16[1024,128]{0,1:T(8,128)(2,1)S(1)} all-gather(bf16[128,128]{0,1:T(8,128)(2,1)S(1)} %get-tuple-element.339), channel_id=1, replica_groups=mesh['fsdp'=4,'seq'=8] {'seq'}, dimensions={0}, use_global_device_ids=true | all-gather | bytes 294912 | tf_op jit(solution)/shard_map/all_gather | solution.py:154
  258.6 13.1 %all_gather.17 = bf16[1024,128]{0,1:T(8,128)(2,1)S(1)} all-gather(bf16[128,128]{0,1:T(8,128)(2,1)S(1)} %get-tuple-element.340), channel_id=1, replica_groups=mesh['fsdp'=4,'seq'=8] {'seq'}, dimensions={0}, use_global_device_ids=true | all-gather | bytes 294912 | tf_op jit(solution)/shard_map/all_gather | solution.py:153
  281.0 5.3 all-to-all-start.1
  290.2 11.4 %all-to-all-done.1 = bf16[128,32,64]{0,2,1:T(8,128)(2,1)} async-done(((bf16[128,32,64]{0,2,1:T(8,128)(2,1)}), bf16[128,32,64]{0,2,1:T(8,128)(2,1)}, u32[]{:S(2)}, u32[]{:S(2)}) %all-to-all-start.1) | async-done | bytes 524320 | tf_op jit(solution)/shard_map/all_to_all | solution.py:149
  307.3 12.4 %while.34 = (s32[]{:T(128)}, f32[4,64,128]{2,1,0:T(8,128)S(1)}, f32[8,4,64,128]{3,2,1,0:T(8,128)S(1)}, f32[8,4,1,1]{1,3,2,0:T(1,128)}, f32[8,4]{1,0:T(8,128)S(1)...) while((s32[]{:T(128)}, f32[4,64,128]{2,1,0:T(8,128)S(1)}, ...), condition=%wide.region_3.4_spmd.clone, body=%wide.region_2.3_spmd.clone.sunk | while | flops 131075 | bytes 656556 | solution.py:73
  329.5 19.8 %all_to_all.83 = bf16[8,2,16384]{2,1,0:T(2,128)(2,1)} all-to-all(bf16[8,2,16384]{2,1,0:T(2,128)(2,1)} %reshape.324), channel_id=1, replica_groups=mesh['fsdp'=4,'seq'=8] {'seq'}, dimensions={0} | all-to-all | bytes 1048576 | tf_op jit(solution)/shard_map/all_to_all | solution.py:192
  369.0 15.3 %all-to-all-done.3 = bf16[128,32,64]{0,2,1:T(8,128)(2,1)} async-done(((bf16[128,32,64]{0,2,1:T(8,128)(2,1)}), bf16[128,32,64]{0,2,1:T(8,128)(2,1)}, u32[]{:S(2)}, u32[]{:S(2)}) %all-to-all-start.3) | async-done | bytes 524320 | tf_op jit(solution)/shard_map/all_to_all | solution.py:205
  393.7 33.2 %while.35 = (s32[]{:T(128)}, f32[4,64,128]{2,1,0:T(8,128)S(1)}, f32[8,4]{1,0:T(8,128)}, f32[8,4,64,128]{3,2,1,0:T(8,128)}, f32[8,4,64,128]{3,2,1,0:T(8,128)}, /*...) while((s32[]{:T(128)}, f32[4,64,128]{2,1,0:T(8,128)S(1)}, ...), condition=%wide.region_8.9_spmd.clone, body=%wide.region_6.8_spmd.clone.sunk | while | flops 196608 | bytes 786668 | solution.py:73
  427.0 6.0 fusion.25
  443.5 5.5 multiply_reduce_fusion.10
  453.6 5.6 fusion.77
  473.5 5.0 reduce_window_sum.23
  479.3 9.1 %all-to-all-done.4 = bf16[8,2,16384]{2,1,0:T(2,128)(2,1)S(1)} async-done(((bf16[8,2,16384]{2,1,0:T(2,128)(2,1)}), bf16[8,2,16384]{2,1,0:T(2,128)(2,1)S(1)}, u32[]{:S(2)}, u32[]{:S(2)}) %all-to-all-start.4) | async-done | bytes 524320 | tf_op jit(solution)/shard_map/all_to_all | solution.py:215
  496.2 17.7 %reduce-scatter.10.cloned.1.call-done = f32[128,128]{0,1:T(8,128)} async-done(((f32[1024,128]{0,1:T(8,128)}), f32[128,128]{0,1:T(8,128)}) %reduce-scatter.10.cloned.1.call-update) | async-done | bytes 65552 | tf_op jit(solution)/shard_map/reduce_scatter | solution.py:220
  514.8 9.2 %fusion.101 = f32[1024,4384]{0,1:T(8,128)} fusion(bf16[128,4384]{0,1:T(8,128)(2,1)S(1)} %constant_dynamic-update-slice_fusion.7, f32[1,128,1024]{2,1,0:T(8,128)S(1)} %copy-done.3, f32[1024]{0:T(1024)S(1)} %copy-done.45, f32[128]{0:T(128)S(1)} %copy-done.81), kind=kOutput, calls=%fused_computation.254 | convolution fusion | flops 1149632512 | bytes 19608064 | tf_op jit(solution)/shard_map/dot_general | solution.py:105
  531.3 5.3 multiply_reduce_fusion.16
  536.6 64.8 %reduce-scatter.14.cloned.1.call-done = f32[512,1024]{1,0:T(8,128)} async-done(((f32[2048,1024]{1,0:T(8,128)}), f32[512,1024]{1,0:T(8,128)}) %reduce-scatter.14.cloned.1.call-update) | async-done | bytes 2097168 | tf_op jit(solution)/shard_map/reduce_scatter | solution.py:238
  601.5 166.5 %reduce-scatter.12.cloned.1.call-done = f32[256,4384]{0,1:T(8,128)} async-done(((f32[1024,4384]{0,1:T(8,128)}), f32[256,4384]{0,1:T(8,128)}) %reduce-scatter.12.cloned.1.call-update) | async-done | bytes 4489232 | tf_op jit(solution)/shard_map/reduce_scatter | solution.py:237
  767.9 70.2 %fusion = f32[256,552]{0,1:T(8,128)S(1)} fusion(f32[256,4384]{0,1:T(8,128)} %reduce-scatter.12.cloned.1.call-done), kind=kCustom, calls=%all-reduce-scatter | all-reduce-scatter fusion | flops 1130497 | bytes 5054976
  840.5 39.7 %all-reduce.31 = (f32[1024]{0:T(1024)}, f32[4,2304]{1,0:T(4,128)}, f32[2304]{0:T(1024)}, f32[32]{0:T(128)}, f32[32]{0:T(128)}, /*index=5*/f32[32]{0:T(128)}, f32[2048]{0:T(1024)}) all-reduce(f32[1024]{0:T(1024)S(1)} %get-tuple-element.282, f32[4,2304]{1,0:T(4,128)S(1)} %pad_maximum_fusion.1, ...), channel_id=1, replica_groups=mesh['fsdp'=4,'seq'=8] {'fsdp','seq'}, use_global_device_ids=true, to_apply=%region_21.22 | all-reduce | flops 14688 | bytes 117504 | tf_op jit(solution)/shard_map/psum | solution.py:261
  (431 shorter events, 178.1 us)
Async XLA Ops:
  7.2 35.7 %all-gather.9.cloned.1.call-start = ((), (), s32[]{:S(2)}) async-start(), calls=%async_computation.18 | async-start | bytes 2543616 | tf_op jit(solution)/shard_map/all_gather | solution.py:133
  7.9 116.4 %all-gather.5.cloned.1.call-start = ((), (), s32[]{:S(2)}) async-start(), calls=%async_computation.11 | async-start | bytes 1179648 | tf_op jit(solution)/shard_map/all_gather | solution.py:134
  45.6 51.0 %collective-permute-start = (bf16[256,4384]{0,1:T(8,128)(2,1)S(1)}, bf16[256,4384]{0,1:T(8,128)(2,1)S(1)}, u32[]{:S(2)}, u32[]{:S(2)}) collective-permute-start(bf16[256,4384]{0,1:T(8,128)(2,1)S(1)} %bitcast.435), channel_id=1, source_target_pairs={{0,24},{8,0},{16,8},{24,16},{1,25},{9,1},{17,9},{25,17},{2,26},{10... | collective-permute-start | bytes 6733832 | tf_op jit(solution)/shard_map/ppermute | solution.py:20
  99.3 132.2 %collective-permute-start.1 = (bf16[512,4384]{0,1:T(8,128)(2,1)}, bf16[512,4384]{0,1:T(8,128)(2,1)}, u32[]{:S(2)}, u32[]{:S(2)}) collective-permute-start(bf16[512,4384]{0,1:T(8,128)(2,1)} %pad_maximum_fusion), channel_id=1, source_target_pairs={{0,16},{8,24},{16,0},{24,8},{1,17},{9,25},{17,1},{25,9},{2,18},{10... | collective-permute-start | bytes 13467656 | tf_op jit(solution)/shard_map/ppermute | solution.py:20
  100.8 256.8 %all-gather.7.cloned.1.call-start = ((), (), s32[]{:S(2)}) async-start(), calls=%async_computation.12 | async-start | bytes 5242880 | tf_op jit(solution)/shard_map/all_gather | solution.py:138
  101.1 187.4 %copy-start.82 = (f32[4]{0:T(128)}, f32[4]{0:T(128)S(1)}, u32[]{:S(2)}) copy-start(f32[4]{0:T(128)S(1)} %dynamic_slice.57) | copy-start | bytes 52
  101.2 224.1 %copy-start.96 = (f32[4]{0:T(128)}, f32[4]{0:T(128)S(1)}, u32[]{:S(2)}) copy-start(f32[4]{0:T(128)S(1)} %dynamic_slice.60) | copy-start | bytes 52
  101.3 201.5 %copy-start.48 = (f32[4,64]{1,0:T(4,128)}, f32[4,64]{1,0:T(4,128)S(1)}, u32[]{:S(2)}) copy-start(f32[4,64]{1,0:T(4,128)S(1)} %get-tuple-element.358) | copy-start | bytes 3076
  101.3 201.5 %copy-start.50 = (f32[4,64]{1,0:T(4,128)}, f32[4,64]{1,0:T(4,128)S(1)}, u32[]{:S(2)}) copy-start(f32[4,64]{1,0:T(4,128)S(1)} %get-tuple-element.359) | copy-start | bytes 3076
  101.3 201.5 %copy-start.52 = (f32[4,64]{1,0:T(4,128)}, f32[4,64]{1,0:T(4,128)S(1)}, u32[]{:S(2)}) copy-start(f32[4,64]{1,0:T(4,128)S(1)} %get-tuple-element.360) | copy-start | bytes 3076
  101.3 201.5 %copy-start.54 = (f32[4,64]{1,0:T(4,128)}, f32[4,64]{1,0:T(4,128)S(1)}, u32[]{:S(2)}) copy-start(f32[4,64]{1,0:T(4,128)S(1)} %get-tuple-element.361) | copy-start | bytes 3076
  101.4 219.3 %copy-start.59 = (pred[128,128]{1,0:T(8,128)(4,1)}, pred[128,128]{1,0:T(8,128)(4,1)S(1)}, u32[]{:S(2)}) copy-start(pred[128,128]{1,0:T(8,128)(4,1)S(1)} %iota_compare_fusion) | copy-start | bytes 49156
  271.8 9.1 %all-to-all-start = ((bf16[128,8,4]{0,2,1:T(4,128)(2,1)}), bf16[128,8,4]{0,2,1:T(4,128)(2,1)S(1)}, u32[]{:S(2)}, u32[]{:S(2)}) async-start(bf16[128,8,4]{0,2,1:T(4,128)(2,1)} %bitcast.12), calls=%async_computation | async-start | bytes 16384 | tf_op jit(solution)/shard_map/all_to_all | solution.py:150
  281.0 20.7 %all-to-all-start.1 = ((bf16[128,32,64]{0,2,1:T(8,128)(2,1)}), bf16[128,32,64]{0,2,1:T(8,128)(2,1)}, u32[]{:S(2)}, u32[]{:S(2)}) async-start(bf16[128,32,64]{0,2,1:T(8,128)(2,1)} %bitcast.445), calls=%async_computation.1 | async-start | bytes 1048576 | tf_op jit(solution)/shard_map/all_to_all | solution.py:149
  364.8 19.5 %all-to-all-start.3 = ((bf16[128,32,64]{0,2,1:T(8,128)(2,1)}), bf16[128,32,64]{0,2,1:T(8,128)(2,1)}, u32[]{:S(2)}, u32[]{:S(2)}) async-start(bf16[128,32,64]{0,2,1:T(8,128)(2,1)} %bitcast.448), calls=%async_computation.3 | async-start | bytes 1048576 | tf_op jit(solution)/shard_map/all_to_all | solution.py:205
  368.9 126.5 %reduce-scatter.8.cloned.1.call-start = ((), (), s32[]{:S(2)}) async-start(), calls=%async_computation.13 | async-start | bytes 589824 | tf_op jit(solution)/shard_map/reduce_scatter | solution.py:219
  450.6 63.3 %reduce-scatter.10.cloned.1.call-start = ((), (), s32[]{:S(2)}) async-start(), calls=%async_computation.14 | async-start | bytes 589824 | tf_op jit(solution)/shard_map/reduce_scatter | solution.py:220
  453.3 148.2 %reduce-scatter.14.cloned.1.call-start = ((), (), s32[]{:S(2)}) async-start(), calls=%async_computation.16 | async-start | bytes 10485760 | tf_op jit(solution)/shard_map/reduce_scatter | solution.py:238
  469.3 19.1 %all-to-all-start.4 = ((bf16[8,2,16384]{2,1,0:T(2,128)(2,1)}), bf16[8,2,16384]{2,1,0:T(2,128)(2,1)S(1)}, u32[]{:S(2)}, u32[]{:S(2)}) async-start(bf16[8,2,16384]{2,1,0:T(2,128)(2,1)} %reshape.326), calls=%async_computation.4 | async-start | bytes 1048576 | tf_op jit(solution)/shard_map/all_to_all | solution.py:215
  488.4 26.4 %all-to-all-start.5 = ((bf16[8,128,4]{1,2,0:T(4,128)(2,1)}), bf16[8,128,4]{1,2,0:T(4,128)(2,1)S(1)}, u32[]{:S(2)}, u32[]{:S(2)}) async-start(bf16[8,128,4]{1,2,0:T(4,128)(2,1)} %bitcast.387), calls=%async_computation.7 | async-start | bytes 16384 | tf_op jit(solution)/shard_map/all_to_all | solution.py:216
  491.8 276.1 %reduce-scatter.12.cloned.1.call-start = ((), (), s32[]{:S(2)}) async-start(), calls=%async_computation.15 | async-start | bytes 22446080 | tf_op jit(solution)/shard_map/reduce_scatter | solution.py:237
  524.1 357.6 %reduce-scatter.16.cloned.1.call-start = ((), (), s32[]{:S(2)}) async-start(), calls=%async_computation.17 | async-start | bytes 2359296 | tf_op jit(solution)/shard_map/reduce_scatter | solution.py:242
  601.5 238.0 %copy-start.17 = (f32[1,128,1024]{2,1,0:T(8,128)S(1)}, f32[1,128,1024]{2,1,0:T(8,128)}, u32[]{:S(2)}) copy-start(f32[1,128,1024]{2,1,0:T(8,128)} %param.25) | copy-start | bytes 1572868
  838.2 42.0 %collective-permute-start.2 = (f32[256,28]{0,1:T(8,128)S(1)}, f32[256,28]{0,1:T(8,128)S(1)}, u32[]{:S(2)}, u32[]{:S(2)}) collective-permute-start(f32[256,28]{0,1:T(8,128)S(1)} %slice.156), channel_id=1, source_target_pairs={{0,1},{1,2},{2,3},{3,4},{4,5},{5,6},{6,7},{8,9},{9,10},{10,11},{11... | collective-permute-start | bytes 86024
  (99 other events, 2761.0 us)
Sparse Core Ops, SparseCore 0:
  9.6 33.2 all-gather.8
  100.9 23.4 all-gather.4
  126.2 85.0 all-gather.6
  450.7 31.5 reduce-scatter.7
  484.4 29.4 reduce-scatter.9
  516.9 84.5 reduce-scatter.13
  604.6 163.2 reduce-scatter.11
  770.8 50.0 reduce-scatter.15
